TPU v7x, 512 devices: a whole 4x8x8 slice. The times are simulated.
512 devices in a mesh: dom: 128 (over y, z, core), scen: 4 (over x).
Axes of the slice: x: 4, y: 8, z: 8, core: 2. Of those that a mesh axis runs over, the one named last changes fastest.
Arguments:
- embedding: bfloat16 [1310720, 256], P(('dom', 'scen')), may hold values from -6 to 6
- scenario_feats: bfloat16 [16, 1310720], P(None, ('dom', 'scen')), may hold values from -6 to 6
- adjacency: bfloat16 [10240, 2, 128, 128], P(('dom', 'scen')), may hold values from -0.3125 to 0.3125
- driver_weight: bfloat16 [1310720, 128], P(('dom', 'scen')), may hold values from -0.3125 to 0.3125
- local_slot: int32 [10240], P(('dom', 'scen')), may hold values from 0 to 79, as said below
- halo_slot: int32 [10240], P(('dom', 'scen')), may hold values from 0 to 15, as said below
- send_rows: int32 [65536, 16], P(('dom', 'scen')), may hold values from 0 to 2559
- send_count: int32 [65536], P(('dom', 'scen')), may hold values from 1 to 16, as said below
- hot_ids: int32 [128], replicated, may hold values from 0 to 1310719, as said below
- first_weight: bfloat16 [512, 256], P('scen'), may hold values from -0.25 to 0.25
- feature_weight: bfloat16 [16, 256], replicated, may hold values from -1.5 to 1.5
- first_bias: float32 [256], replicated, may hold values from -3 to 3
- second_weight: bfloat16 [256, 256], P('scen'), may hold values from -0.375 to 0.375
- second_bias: float32 [256], replicated, may hold values from -3 to 3
Outputs:
- updated: bfloat16 [1310720, 256], P(('dom', 'scen'))
Inputs may be any that keep to these rules, and one draw needn't show every extreme that they name: `local_slot`: the 20 entries of one device are distinct and name exactly 5 tiles of each device of its partition; values s * 20 to s * 20 + 19 are tiles of scen index s. `halo_slot`: the entries of one device name every halo tile at least once. `send_count`: every device has a partition to which it sends 16 pins. `hot_ids`: no device holds more than 1 of them, and some device holds exactly that many.
All inputs are finite; a program needn't handle non-finite values.
Results may differ from a plain program's by a relative error of at most 0.0038.
Values may be sent and summed in bfloat16 or wider, within the bound.
No kernel may reach another device: no remote copies, remote signals or barrier semaphores. Data moves between devices by JAX's collectives and lax.ppermute only.
A program may use at most 64 MiB of HBM per device.

v0:
```python
import jax
import jax.numpy as jnp
from jax import lax
from jax.sharding import PartitionSpec as P


def per_device(
    embedding,
    scenario_feats,
    adjacency,
    driver_weight,
    local_slot,
    halo_slot,
    send_rows,
    send_count,
    hot_ids,
    first_weight,
    feature_weight,
    first_bias,
    second_weight,
    second_bias,
):
    rows, width = embedding.shape
    tile = adjacency.shape[-1]
    tiles = rows // tile
    groups = lax.axis_size("scen")
    partition = lax.all_gather(embedding, "scen", axis=0, tiled=True)
    local_tiles = partition.reshape(groups * tiles, tile, width)[local_slot]
    slots_per_peer = send_rows.shape[1]
    live = jnp.arange(slots_per_peer, dtype=jnp.int32)[None, :] < send_count[:, None]
    outgoing_rows = jnp.where(
        live[:, :, None], embedding[send_rows], jnp.zeros((), embedding.dtype)
    )
    incoming = lax.all_to_all(outgoing_rows, "dom", split_axis=0, concat_axis=0, tiled=True)
    halo_tiles = incoming.reshape(-1, tile, width)[halo_slot]
    myself = lax.axis_index(("dom", "scen"))
    owner = hot_ids // rows
    within = hot_ids - owner * rows
    mine = jnp.where(
        (owner == myself)[:, None], embedding[within].astype(jnp.float32), jnp.float32(0.0)
    )
    drivers = lax.psum(mine, ("dom", "scen")).astype(jnp.bfloat16)
    summed = jnp.einsum(
        "tij,tjc->tic", adjacency[:, 0], local_tiles, preferred_element_type=jnp.float32
    )
    summed = summed + jnp.einsum(
        "tij,tjc->tic", adjacency[:, 1], halo_tiles, preferred_element_type=jnp.float32
    )
    summed = summed.reshape(rows, width) + jnp.dot(
        driver_weight, drivers, preferred_element_type=jnp.float32
    )
    aggregate = summed.astype(jnp.bfloat16)
    joined = jnp.concatenate([embedding, aggregate], axis=1)
    starting = (
        jnp.dot(scenario_feats.T, feature_weight, preferred_element_type=jnp.float32) + first_bias
    )
    columns = joined
    inner = starting + jnp.dot(
        columns,
        lax.all_gather(first_weight, "scen", axis=0, tiled=True),
        preferred_element_type=jnp.float32,
    )
    activated = jax.nn.gelu(inner, approximate=False).astype(jnp.bfloat16)
    residual = embedding.astype(jnp.float32) + second_bias
    columns = activated
    result = residual + jnp.dot(
        columns,
        lax.all_gather(second_weight, "scen", axis=0, tiled=True),
        preferred_element_type=jnp.float32,
    )
    return result.astype(jnp.bfloat16)


def solution(mesh):
    return jax.shard_map(
        per_device,
        mesh=mesh,
        in_specs=(
            P(("dom", "scen"), None),
            P(None, ("dom", "scen")),
            P(("dom", "scen"), None, None, None),
            P(("dom", "scen"), None),
            P(("dom", "scen")),
            P(("dom", "scen")),
            P(("dom", "scen"), None),
            P(("dom", "scen")),
            P(),
            P("scen", None),
            P(),
            P(),
            P("scen", None),
            P(),
        ),
        out_specs=P(("dom", "scen"), None),
        check_vma=False,
    )
```

profile of v0, /device:TPU:8, one launch (start us, length us, event | category | flops | bytes accessed | tf_op | source)
XLA Modules:
  0.0 204.4 jit_solution(11013594092646320890)
XLA Ops:
  6.5 0.7 all-gather.2.cloned.1.call-update
  7.3 0.7 compare_select_fusion
  8.0 0.1 copy.18
  8.2 7.5 %gather_fusion.1 = bf16[2048,256]{1,0:T(8,128)(2,1)S(1)} fusion(bf16[2560,256]{1,0:T(8,128)(2,1)S(1)} %copy-done.1, s32[2048]{0:T(1024)S(1)} %broadcast_clamp_fusion), kind=kCustom, calls=%fused_computation.1 | custom fusion | bytes 2105344 | tf_op jit(solution)/shard_map/gather | solution.py:32
  15.7 0.1 iota_compare_fusion
  15.8 1.2 broadcast_select_fusion
  17.1 17.4 %all-to-all-start = ((bf16[128,16,256]{2,1,0:T(8,128)(2,1)}), bf16[128,16,256]{2,1,0:T(8,128)(2,1)S(1)}, u32[]{:S(2)}, u32[]{:S(2)}) async-start(bf16[128,16,256]{2,1,0:T(8,128)(2,1)} %broadcast_select_fusion), calls=%async_computation | async-start | bytes 2097152 | tf_op jit(solution)/shard_map/all_to_all | solution.py:34
  34.5 0.8 gather_fusion.3
  35.3 0.1 convert_select_fusion
  35.4 114.3 %all-reduce.1 = bf16[128,256]{1,0:T(8,128)(2,1)S(1)} all-reduce(f32[128,256]{1,0:T(8,128)S(1)} %convert_select_fusion), channel_id=1, replica_groups=mesh['dom'=128,'scen'=4] {'dom','scen'}, use_global_device_ids=true, to_apply=%region_0.1 | all-reduce | flops 32768 | bytes 196608 | tf_op jit(solution)/shard_map/psum | solution.py:42
  149.8 12.2 %all_gather.11 = bf16[256,256]{1,0:T(8,128)(2,1)S(1)} all-gather(bf16[64,256]{1,0:T(8,128)(2,1)} %param.26), channel_id=1, replica_groups=mesh['dom'=128,'scen'=4] {'scen'}, dimensions={0}, use_global_device_ids=true | all-gather | bytes 163840 | tf_op jit(solution)/shard_map/all_gather | solution.py:68
  162.0 13.2 %all_gather.10 = bf16[512,256]{1,0:T(8,128)(2,1)} all-gather(bf16[128,256]{1,0:T(8,128)(2,1)S(1)} %copy-done.5), channel_id=1, replica_groups=mesh['dom'=128,'scen'=4] {'scen'}, dimensions={0}, use_global_device_ids=true | all-gather | bytes 327680 | tf_op jit(solution)/shard_map/all_gather | solution.py:60
  175.1 0.7 compare_select_fusion.2
  175.8 0.7 compare_select_fusion.3
  176.4 0.6 pad_clamp_fusion.2
  177.0 2.7 %convolution_add_fusion.2 = f32[2560,256]{1,0:T(8,128)} fusion(bf16[16,2560]{1,0:T(8,128)(2,1)S(1)} %copy-done.4, bf16[16,256]{1,0:T(8,128)(2,1)} %param.24, f32[256]{0:T(256)} %param.25), kind=kOutput, calls=%fused_computation.6 | convolution fusion | flops 21626880 | bytes 2712576 | tf_op jit(solution)/shard_map/dot_general | solution.py:55
  179.8 1.8 gather_fusion.2
  181.5 3.2 %gather_fusion = bf16[20,128,256]{2,1,0:T(8,128)(2,1)S(1)} fusion(bf16[80,128,256]{2,1,0:T(8,128)(2,1)} %bitcast.33, s32[1024]{0:T(1024)} %pad_clamp_fusion.2), kind=kCustom, calls=%fused_computation | custom fusion | bytes 2621520 | tf_op jit(solution)/shard_map/gather | solution.py:28
  184.8 1.7 fusion.52
  186.6 0.1 copy-done.3
  186.7 0.5 convolution_add_fusion.3
  187.2 0.5 fusion.1
  187.7 0.2 copy-done.8
  187.9 9.7 %fusion.2 = bf16[2560,256]{1,0:T(8,128)(2,1)} fusion(bf16[256,256]{1,0:T(8,128)(2,1)S(1)} %all_gather.11, bf16[2560,256]{1,0:T(8,128)(2,1)S(1)} %copy-done.1, f32[256]{0:T(256)S(1)} %copy-done.8, f32[2560,256]{1,0:T(8,128)} %convolution_add_fusion.2, bf16[512,256]{1,0:T(8,128)(2,1)} %all_gather.10, bf16[2560,256]{1,0:T(8,128)(2,1)S(1)} %fusion.1), kind=kOutput, calls=%fused_computation.11 | convolution fusion | flops 1057751040 | bytes 6947840 | tf_op jit(solution)/shard_map/dot_general | solution.py:66
  (25 shorter events, 0.2 us)
Async XLA Ops:
  6.5 180.7 %copy-start = (bf16[2560,128]{1,0:T(8,128)(2,1)S(1)}, bf16[2560,128]{1,0:T(8,128)(2,1)}, u32[]{:S(2)}) copy-start(bf16[2560,128]{1,0:T(8,128)(2,1)} %param.17) | copy-start | bytes 1966084
  6.5 1.6 copy-start.1
  6.5 175.0 %all-gather.2.cloned.1.call-start = ((), (), s32[]{:S(2)}) async-start(), calls=%async_computation.1 | async-start | bytes 6553600 | tf_op jit(solution)/shard_map/all_gather | solution.py:27
  8.2 7.5 %copy-start.6 = (s32[128]{0:T(128)S(1)}, s32[128]{0:T(128)}, u32[]{:S(2)}) copy-start(s32[128]{0:T(128)} %param.21) | copy-start | bytes 1540
  15.7 18.8 %copy-start.7 = (s32[128]{0:T(128)S(1)}, s32[128]{0:T(128)}, u32[]{:S(2)}) copy-start(s32[128]{0:T(128)} %param.22) | copy-start | bytes 1540
  15.8 146.2 %copy-start.5 = (bf16[128,256]{1,0:T(8,128)(2,1)S(1)}, bf16[128,256]{1,0:T(8,128)(2,1)}, u32[]{:S(2)}) copy-start(bf16[128,256]{1,0:T(8,128)(2,1)} %param.23) | copy-start | bytes 196612
  15.8 161.2 %copy-start.4 = (bf16[16,2560]{1,0:T(8,128)(2,1)S(1)}, bf16[16,2560]{1,0:T(8,128)(2,1)}, u32[]{:S(2)}) copy-start(bf16[16,2560]{1,0:T(8,128)(2,1)} %param.15) | copy-start | bytes 245764
  17.1 162.7 %all-to-all-start = ((bf16[128,16,256]{2,1,0:T(8,128)(2,1)}), bf16[128,16,256]{2,1,0:T(8,128)(2,1)S(1)}, u32[]{:S(2)}, u32[]{:S(2)}) async-start(bf16[128,16,256]{2,1,0:T(8,128)(2,1)} %broadcast_select_fusion), calls=%async_computation | async-start | bytes 2097152 | tf_op jit(solution)/shard_map/all_to_all | solution.py:34
  184.8 1.8 copy-start.2
  184.8 1.9 copy-start.3
  187.2 0.7 copy-start.8
Sparse Core Ops, SparseCore 0:
  9.5 66.8 all-gather.1
where the time goes:
time: 205 us; the launch traced here: 204 us
  blocking collectives  140 us (68%)
  starting transfers between devices  17.4 us (8%)
  matrix products  15.1 us (7%)
  local copies, waits for them, and re-layouts  13.9 us (7%)
  between operations  13.6 us (7%)
  other arithmetic  4.05 us (2%)
    psum x1, blocking collectives, per_device(): drivers = lax.psum(mine, ('dom', 'scen')).astype(jnp.bfloat16)  114 us
    all_to_all x1, starting transfers between devices, per_device(): lax.all_to_all(outgoing_rows, 'dom', split_axis=0, concat_axis=0, tiled=T...  17.4 us
    all_gather x1, blocking collectives, per_device(): lax.all_gather(first_weight, 'scen', axis=0, tiled=True)  13.2 us
    all_gather x1, blocking collectives, per_device(): lax.all_gather(second_weight, 'scen', axis=0, tiled=True)  12.2 us
    dot_general x1, matrix products, per_device(): jnp.dot(columns, lax.all_gather(second_weight, 'scen', axis=0, tiled=True...  9.68 us
    gather x1, local copies, waits for them, and re-layouts, per_device(): embedding[send_rows]  7.5 us
  transfers between devices with their start and end apart: 2, of which 0 were waited for; matrix products, arithmetic and copies ran while one was open for 8% of the time, Pallas kernels for 0%

commit v1 on v0

--- a/solution.py
+++ b/solution.py
@@ -57,7 +57,9 @@
     columns = joined
     inner = starting + jnp.dot(
         columns,
-        lax.all_gather(first_weight, "scen", axis=0, tiled=True),
+        jnp.concatenate(
+            lax.all_to_all(jnp.stack([first_weight] * lax.axis_size("scen")), "scen", 0, 0), axis=0
+        ),
         preferred_element_type=jnp.float32,
     )
     activated = jax.nn.gelu(inner, approximate=False).astype(jnp.bfloat16)

time: 205 us -> 198 us (0.966)
  the two profiles are of different devices: /device:TPU:8 before, /device:TPU:2 now
where the time goes in v1:
time: 198 us; the launch traced here: 197 us
  blocking collectives  126 us (64%)
  starting transfers between devices  23.1 us (12%)
  matrix products  15.1 us (8%)
  local copies, waits for them, and re-layouts  14.6 us (7%)
  between operations  13.6 us (7%)
  other arithmetic  4.06 us (2%)
    psum x1, blocking collectives, per_device(): drivers = lax.psum(mine, ('dom', 'scen')).astype(jnp.bfloat16)  115 us
    all_to_all x1, starting transfers between devices, per_device(): lax.all_to_all(outgoing_rows, 'dom', split_axis=0, concat_axis=0, tiled=T...  17.9 us
    all_gather x1, blocking collectives, per_device(): lax.all_gather(second_weight, 'scen', axis=0, tiled=True)  11 us
    dot_general x1, matrix products, per_device(): jnp.dot(columns, lax.all_gather(second_weight, 'scen', axis=0, tiled=True...  9.68 us
    gather x1, local copies, waits for them, and re-layouts, per_device(): embedding[send_rows]  7.5 us
    all_to_all x1, starting transfers between devices, per_device(): lax.all_to_all(jnp.stack([first_weight] * lax.axis_size('scen')), 'scen',...  5.19 us
  transfers between devices with their start and end apart: 3, of which 0 were waited for; matrix products, arithmetic and copies ran while one was open for 12% of the time, Pallas kernels for 0%

profile of v1, /device:TPU:2, one launch (start us, length us, event | category | flops | bytes accessed | tf_op | source)
XLA Modules:
  0.0 197.1 jit_solution(6666367363958307642)
XLA Ops:
  6.5 0.7 all-gather.2.cloned.1.call-update
  7.3 0.7 compare_select_fusion
  8.0 0.1 copy.18
  8.2 7.5 %gather_fusion.1 = bf16[2048,256]{1,0:T(8,128)(2,1)S(1)} fusion(bf16[2560,256]{1,0:T(8,128)(2,1)S(1)} %copy-done.1, s32[2048]{0:T(1024)S(1)} %broadcast_clamp_fusion), kind=kCustom, calls=%fused_computation.1 | custom fusion | bytes 2105344 | tf_op jit(solution)/shard_map/gather | solution.py:32
  15.7 0.1 iota_compare_fusion
  15.8 1.2 broadcast_select_fusion
  17.0 17.9 %all-to-all-start = ((bf16[128,16,256]{2,1,0:T(8,128)(2,1)}), bf16[128,16,256]{2,1,0:T(8,128)(2,1)S(1)}, u32[]{:S(2)}, u32[]{:S(2)}) async-start(bf16[128,16,256]{2,1,0:T(8,128)(2,1)} %broadcast_select_fusion), calls=%async_computation | async-start | bytes 2097152 | tf_op jit(solution)/shard_map/all_to_all | solution.py:34
  35.1 0.8 gather_fusion.3
  36.0 114.9 %all-reduce.1 = bf16[128,256]{1,0:T(8,128)(2,1)S(1)} all-reduce(f32[128,256]{1,0:T(8,128)S(1)} %convert_select_fusion), channel_id=1, replica_groups=mesh['dom'=128,'scen'=4] {'dom','scen'}, use_global_device_ids=true, to_apply=%region_0.1 | all-reduce | flops 32768 | bytes 196608 | tf_op jit(solution)/shard_map/psum | solution.py:42
  150.9 11.0 %all_gather.7 = bf16[256,256]{1,0:T(8,128)(2,1)S(1)} all-gather(bf16[64,256]{1,0:T(8,128)(2,1)} %param.26), channel_id=1, replica_groups=mesh['dom'=128,'scen'=4] {'scen'}, dimensions={0}, use_global_device_ids=true | all-gather | bytes 163840 | tf_op jit(solution)/shard_map/all_gather | solution.py:70
  161.9 0.7 compare_select_fusion.2
  162.6 0.7 compare_select_fusion.3
  163.2 0.6 pad_clamp_fusion.2
  163.8 2.7 %convolution_add_fusion.2 = f32[2560,256]{1,0:T(8,128)} fusion(bf16[16,2560]{1,0:T(8,128)(2,1)S(1)} %copy-done.4, bf16[16,256]{1,0:T(8,128)(2,1)} %param.24, f32[256]{0:T(256)} %param.25), kind=kOutput, calls=%fused_computation.6 | convolution fusion | flops 21626880 | bytes 2712576 | tf_op jit(solution)/shard_map/dot_general | solution.py:55
  166.6 0.7 stack.2
  167.3 5.2 %all-to-all-start.1 = ((bf16[4,128,256]{2,1,0:T(8,128)(2,1)}), bf16[4,128,256]{2,1,0:T(8,128)(2,1)}, u32[]{:S(2)}, u32[]{:S(2)}) async-start(bf16[4,128,256]{2,1,0:T(8,128)(2,1)} %stack.2), calls=%async_computation.1 | async-start | bytes 524288 | tf_op jit(solution)/shard_map/all_to_all | solution.py:61
  172.5 1.8 gather_fusion.2
  174.3 3.2 %gather_fusion = bf16[20,128,256]{2,1,0:T(8,128)(2,1)S(1)} fusion(bf16[80,128,256]{2,1,0:T(8,128)(2,1)} %bitcast.34, s32[1024]{0:T(1024)} %pad_clamp_fusion.2), kind=kCustom, calls=%fused_computation | custom fusion | bytes 2621520 | tf_op jit(solution)/shard_map/gather | solution.py:28
  177.5 1.7 fusion.52
  179.3 0.1 copy-done.3
  179.4 0.5 convolution_add_fusion.3
  179.9 0.5 fusion.1
  180.5 0.2 copy-done.8
  180.6 9.7 %fusion.2 = bf16[2560,256]{1,0:T(8,128)(2,1)} fusion(bf16[256,256]{1,0:T(8,128)(2,1)S(1)} %all_gather.7, bf16[2560,256]{1,0:T(8,128)(2,1)S(1)} %copy-done.1, f32[256]{0:T(256)S(1)} %copy-done.8, f32[2560,256]{1,0:T(8,128)} %convolution_add_fusion.2, bf16[512,256]{1,0:T(8,128)(2,1)} %bitcast.8, bf16[2560,256]{1,0:T(8,128)(2,1)S(1)} %fusion.1), kind=kOutput, calls=%fused_computation.11 | convolution fusion | flops 1057751040 | bytes 6947840 | tf_op jit(solution)/shard_map/dot_general | solution.py:68
  (27 shorter events, 0.3 us)
Async XLA Ops:
  6.5 173.4 %copy-start = (bf16[2560,128]{1,0:T(8,128)(2,1)S(1)}, bf16[2560,128]{1,0:T(8,128)(2,1)}, u32[]{:S(2)}) copy-start(bf16[2560,128]{1,0:T(8,128)(2,1)} %param.17) | copy-start | bytes 1966084
  6.5 1.6 copy-start.1
  6.5 167.7 %all-gather.2.cloned.1.call-start = ((), (), s32[]{:S(2)}) async-start(), calls=%async_computation.2 | async-start | bytes 6553600 | tf_op jit(solution)/shard_map/all_gather | solution.py:27
  8.2 7.5 %copy-start.6 = (s32[128]{0:T(128)S(1)}, s32[128]{0:T(128)}, u32[]{:S(2)}) copy-start(s32[128]{0:T(128)} %param.21) | copy-start | bytes 1540
  15.7 19.3 %copy-start.7 = (s32[128]{0:T(128)S(1)}, s32[128]{0:T(128)}, u32[]{:S(2)}) copy-start(s32[128]{0:T(128)} %param.22) | copy-start | bytes 1540
  15.8 148.1 %copy-start.4 = (bf16[16,2560]{1,0:T(8,128)(2,1)S(1)}, bf16[16,2560]{1,0:T(8,128)(2,1)}, u32[]{:S(2)}) copy-start(bf16[16,2560]{1,0:T(8,128)(2,1)} %param.15) | copy-start | bytes 245764
  17.0 149.5 %copy-start.5 = (bf16[128,256]{1,0:T(8,128)(2,1)S(1)}, bf16[128,256]{1,0:T(8,128)(2,1)}, u32[]{:S(2)}) copy-start(bf16[128,256]{1,0:T(8,128)(2,1)} %param.23) | copy-start | bytes 196612
  17.0 149.5 %all-to-all-start = ((bf16[128,16,256]{2,1,0:T(8,128)(2,1)}), bf16[128,16,256]{2,1,0:T(8,128)(2,1)S(1)}, u32[]{:S(2)}, u32[]{:S(2)}) async-start(bf16[128,16,256]{2,1,0:T(8,128)(2,1)} %broadcast_select_fusion), calls=%async_computation | async-start | bytes 2097152 | tf_op jit(solution)/shard_map/all_to_all | solution.py:34
  167.3 13.1 %all-to-all-start.1 = ((bf16[4,128,256]{2,1,0:T(8,128)(2,1)}), bf16[4,128,256]{2,1,0:T(8,128)(2,1)}, u32[]{:S(2)}, u32[]{:S(2)}) async-start(bf16[4,128,256]{2,1,0:T(8,128)(2,1)} %stack.2), calls=%async_computation.1 | async-start | bytes 524288 | tf_op jit(solution)/shard_map/all_to_all | solution.py:61
  177.5 1.8 copy-start.2
  177.5 1.9 copy-start.3
  179.9 0.7 copy-start.8
Sparse Core Ops, SparseCore 0:
  9.5 66.4 all-gather.1
